TPU v7x, 256 devices: a whole 4x4x8 slice. The times are simulated.
256 devices in a mesh: dp: 4 (over x), context: 32 (over y, z), head: 2 (over core).
Axes of the slice: x: 4, y: 4, z: 8, core: 2. Of those that a mesh axis runs over, the one named last changes fastest.
Arguments:
- tokens: bfloat16 [4, 2, 4096, 4096], P('dp', None, 'context', 'head'), may hold values from -7 to 7
- queries: bfloat16 [4, 2, 4096, 2048], P('dp', None, 'context', 'head'), may hold values from -160 to 160
- grad_out: bfloat16 [4, 2, 4096, 2048], P('dp', None, 'context', 'head'), may hold values from -6 to 6
- w_key: bfloat16 [4096, 256], P('context', 'head'), may hold values from -0.09375 to 0.09375
- w_value: bfloat16 [4096, 256], P('context', 'head'), may hold values from -0.09375 to 0.09375
- block_len: int32 [4], P('dp'), may hold values from 8 to 32, as said below
Outputs:
- grad_query: bfloat16 [4, 2, 4096, 2048], P('dp', None, 'context', 'head')
- grad_x: bfloat16 [4, 2, 4096, 4096], P('dp', None, 'context', 'head')
- grad_wkey: float32 [4096, 256], P('context', 'head')
- grad_wvalue: float32 [4096, 256], P('context', 'head')
Inputs may be any that keep to these rules, and one draw needn't show every extreme that they name: `block_len`: each entry is 8, 16 or 32.
All inputs are finite; a program needn't handle non-finite values.
Results may differ from a plain program's by a relative error of at most 0.025.
Values may be sent and summed in bfloat16 or wider, within the bound.
No kernel may reach another device: no remote copies, remote signals or barrier semaphores. Data moves between devices by JAX's collectives and lax.ppermute only.
A program may use at most 64 MiB of HBM per device.

v0:
```python
import math
import jax
import jax.numpy as jnp
from jax import lax
from jax.sharding import Mesh
from jax.sharding import PartitionSpec as P

HEAD_DIM = 128
CONTEXT = ("context_0", "context_1")
masked_score = -1e30


def joined_along(tiles, dim):
    lengths = list(tiles.shape[1:])
    lengths[dim] *= tiles.shape[0]
    return jnp.moveaxis(tiles, 0, dim).reshape(lengths)


def sent_to_all(array, axis):
    copies = jnp.broadcast_to(array, (lax.axis_size(axis), *array.shape))
    return lax.all_to_all(copies, axis, split_axis=0, concat_axis=0, tiled=True)


def gather_directly(array, axis, dim):
    return joined_along(sent_to_all(array, axis), dim)


def summed_rows(array, axes, dim):
    for axis in axes:
        array = lax.psum_scatter(array, axis, scatter_dimension=dim, tiled=True)
    return array


def split_up(array, dim, peers):
    lengths = array.shape
    tiles = array.reshape(*lengths[:dim], peers, lengths[dim] // peers, *lengths[dim + 1 :])
    return jnp.moveaxis(tiles, dim, 0)


def summed_on_arrival(array, axis, dim):
    peers = lax.axis_size(axis)
    tiles = lax.all_to_all(split_up(array, dim, peers), axis, 0, 0, tiled=True)
    return jnp.sum(tiles.astype(jnp.float32), axis=0)


def sum_by_axis(terms, axes):
    so_far = terms.astype(jnp.bfloat16)
    for axis in axes:
        so_far = lax.psum_scatter(so_far, axis, scatter_dimension=0, tiled=True)
    return so_far.astype(jnp.float32)


def over_copies(array, axis):
    everything = sent_to_all(array, axis)
    return jnp.sum(everything.astype(jnp.float32), axis=0)


def score_block(query_rows, key_rows, score_scale):
    return (
        jnp.einsum("ikgd,jkd->kgij", query_rows, key_rows, preferred_element_type=jnp.float32)
        * score_scale
    )


def visible_mask(query_pos, key_pos, block_size, strict):
    query_block = query_pos // block_size
    key_block = key_pos // block_size
    if strict:
        return key_block[None, :] < query_block[:, None]
    return key_block[None, :] <= query_block[:, None]


def forward_step(carried, query_rows, key_rows, value_rows, allowed_mask, score_scale):
    row_peak, row_total, weighted = carried
    logits = jnp.where(allowed_mask, score_block(query_rows, key_rows, score_scale), masked_score)
    new_peak = jnp.maximum(row_peak, jnp.max(logits, axis=-1))
    shrink = jnp.exp(row_peak - new_peak)
    weights = jnp.where(allowed_mask, jnp.exp(logits - new_peak[..., None]), 0.0)
    row_total = row_total * shrink + jnp.sum(weights, axis=-1)
    update = jnp.einsum(
        "kgij,jkd->kgid",
        weights.astype(jnp.bfloat16),
        value_rows,
        preferred_element_type=jnp.float32,
    )
    return (new_peak, row_total, weighted * shrink[..., None] + update)


def backward_step(
    query_rows, grad_rows, key_rows, value_rows, allowed_mask, log_total, row_delta, score_scale
):
    logits = jnp.where(allowed_mask, score_block(query_rows, key_rows, score_scale), masked_score)
    probs = jnp.exp(logits - log_total[..., None])
    probs_half = probs.astype(jnp.bfloat16)
    grad_probs = jnp.einsum(
        "ikgd,jkd->kgij", grad_rows, value_rows, preferred_element_type=jnp.float32
    )
    grad_logits = (probs * (grad_probs - row_delta[..., None])).astype(jnp.bfloat16)
    grad_rows_query = jnp.einsum(
        "kgij,jkd->ikgd", grad_logits, key_rows, preferred_element_type=jnp.float32
    )
    grad_key = (
        jnp.einsum("kgij,ikgd->jkd", grad_logits, query_rows, preferred_element_type=jnp.float32)
        * score_scale
    )
    grad_value = jnp.einsum(
        "kgij,ikgd->jkd", probs_half, grad_rows, preferred_element_type=jnp.float32
    )
    return (grad_rows_query, grad_key, grad_value)


def finish_rows(carried, grad_rows):
    row_peak, row_total, weighted = carried
    outputs = weighted / row_total[..., None]
    row_delta = jnp.einsum("ikgd,kgid->kgi", grad_rows.astype(jnp.float32), outputs)
    return (row_peak + jnp.log(row_total), row_delta)


def per_device(tokens, queries, grad_out, w_key, w_value, block_len):
    cycle_size = lax.axis_size(CONTEXT)
    my_index = lax.axis_index(CONTEXT)
    shard_rows = tokens.shape[2]
    kv_width = w_key.shape[1]
    kv_local = kv_width // HEAD_DIM
    query_width = queries.shape[3]
    group_size = query_width // HEAD_DIM // kv_local
    score_scale = 1.0 / math.sqrt(HEAD_DIM)
    block_size = block_len[0]
    local_pos = lax.iota(jnp.int32, shard_rows)
    span_rows = min(cycle_size * shard_rows, max(512, shard_rows))
    full_tokens = gather_directly(tokens[0].reshape(2 * shard_rows, tokens.shape[3]), "head", 1)
    weight_pair = jnp.concatenate([w_key, w_value], axis=1)
    columns = full_tokens
    projected = jnp.dot(
        columns,
        lax.all_gather(weight_pair, CONTEXT, axis=0, tiled=True),
        preferred_element_type=jnp.float32,
    ).astype(jnp.bfloat16)
    clean_pairs = projected[:shard_rows]
    q_clean = queries[0, 0].reshape(shard_rows, kv_local, group_size, HEAD_DIM)
    g_clean = grad_out[0, 0].reshape(shard_rows, kv_local, group_size, HEAD_DIM)
    noisy_bundle = jnp.concatenate([queries[0, 1], grad_out[0, 1], projected[shard_rows:]], axis=1)
    q_noisy = noisy_bundle[:, :query_width].reshape(shard_rows, kv_local, group_size, HEAD_DIM)
    g_noisy = noisy_bundle[:, query_width : 2 * query_width].reshape(
        shard_rows, kv_local, group_size, HEAD_DIM
    )
    k_noisy = noisy_bundle[:, 2 * query_width : 2 * query_width + kv_width].reshape(
        shard_rows, kv_local, HEAD_DIM
    )
    v_noisy = noisy_bundle[:, 2 * query_width + kv_width :].reshape(shard_rows, kv_local, HEAD_DIM)
    clean_pos = my_index * shard_rows + local_pos
    noisy_pos = my_index * shard_rows + local_pos
    own_block = local_pos // block_size
    same_block = own_block[None, :] == own_block[:, None]
    clean_limit = (my_index + 1) * shard_rows
    noisy_limit = (my_index + 1) * shard_rows
    state_shape = (kv_local, group_size, shard_rows)
    empty_state = (
        jnp.full(state_shape, masked_score, jnp.float32),
        jnp.zeros(state_shape, jnp.float32),
        jnp.zeros(state_shape + (HEAD_DIM,), jnp.float32),
    )
    noisy_start = forward_step(empty_state, q_noisy, k_noisy, v_noisy, same_block, score_scale)
    block_turns = (jnp.maximum(clean_limit, noisy_limit) + span_rows - 1) // span_rows

    def split_pairs(pair_rows):
        count_rows = pair_rows.shape[0]
        key_rows = pair_rows[:, :kv_width].reshape(count_rows, kv_local, HEAD_DIM)
        value_rows = pair_rows[:, kv_width:].reshape(count_rows, kv_local, HEAD_DIM)
        return (key_rows, value_rows)

    carried = (empty_state, noisy_start)
    pair_rows = gather_directly(clean_pairs, CONTEXT, 0)
    first_row = jnp.int32(0)
    key_rows, value_rows = split_pairs(pair_rows)
    key_pos = lax.iota(jnp.int32, pair_rows.shape[0])
    clean_mask = visible_mask(clean_pos, key_pos, block_size, False)
    noisy_mask = visible_mask(noisy_pos, key_pos, block_size, True)

    def clean_update():
        return forward_step(carried[0], q_clean, key_rows, value_rows, clean_mask, score_scale)

    def clean_keep():
        return carried[0]

    def noisy_update():
        return forward_step(carried[1], q_noisy, key_rows, value_rows, noisy_mask, score_scale)

    def noisy_keep():
        return carried[1]

    clean_state = lax.cond(first_row < clean_limit, clean_update, clean_keep)
    noisy_state = lax.cond(first_row < noisy_limit, noisy_update, noisy_keep)
    clean_lse, clean_delta = finish_rows(clean_state, g_clean)
    noisy_lse, noisy_delta = finish_rows(noisy_state, g_noisy)
    pairs_back = lax.all_gather(clean_pairs, CONTEXT, axis=0, tiled=True)
    query_zero = jnp.zeros((shard_rows, kv_local, group_size, HEAD_DIM), jnp.float32)

    def backward_turn(turn_index, carried):
        query_grads, pair_total = carried
        first_row = turn_index * span_rows
        pair_rows = lax.dynamic_slice_in_dim(pairs_back, first_row, span_rows, 0)
        key_rows, value_rows = split_pairs(pair_rows)
        key_pos = first_row + lax.iota(jnp.int32, span_rows)
        clean_mask = visible_mask(clean_pos, key_pos, block_size, False)
        noisy_mask = visible_mask(noisy_pos, key_pos, block_size, True)
        pair_zero = jnp.zeros((span_rows, kv_local, HEAD_DIM), jnp.float32)

        def clean_work():
            return backward_step(
                q_clean,
                g_clean,
                key_rows,
                value_rows,
                clean_mask,
                clean_lse,
                clean_delta,
                score_scale,
            )

        def noisy_work():
            return backward_step(
                q_noisy,
                g_noisy,
                key_rows,
                value_rows,
                noisy_mask,
                noisy_lse,
                noisy_delta,
                score_scale,
            )

        def no_work():
            return (query_zero, pair_zero, pair_zero)

        clean_dq, clean_dk, clean_dv = lax.cond(first_row < clean_limit, clean_work, no_work)
        noisy_dq, noisy_dk, noisy_dv = lax.cond(first_row < noisy_limit, noisy_work, no_work)
        pair_grads = jnp.concatenate(
            [
                (clean_dk + noisy_dk).reshape(span_rows, kv_width),
                (clean_dv + noisy_dv).reshape(span_rows, kv_width),
            ],
            axis=1,
        )
        previous = lax.dynamic_slice_in_dim(pair_total, first_row, span_rows, 0)
        pair_total = lax.dynamic_update_slice_in_dim(
            pair_total, previous + pair_grads, first_row, 0
        )
        return ((query_grads[0] + clean_dq, query_grads[1] + noisy_dq), pair_total)

    pair_empty = jnp.zeros((cycle_size * shard_rows, 2 * kv_width), jnp.float32)
    query_grads, pair_total = lax.fori_loop(
        0, block_turns, backward_turn, ((query_zero, query_zero), pair_empty)
    )
    clean_pair_grads = (
        summed_rows(pair_total.astype(jnp.bfloat16), CONTEXT, 0)
        .astype(jnp.float32)
        .astype(jnp.bfloat16)
    )
    own_dq, own_dk, own_dv = backward_step(
        q_noisy, g_noisy, k_noisy, v_noisy, same_block, noisy_lse, noisy_delta, score_scale
    )
    dq_clean = (query_grads[0] * score_scale).astype(jnp.bfloat16).reshape(shard_rows, query_width)
    dq_noisy = (
        ((query_grads[1] + own_dq) * score_scale)
        .astype(jnp.bfloat16)
        .reshape(shard_rows, query_width)
    )
    noisy_pair = jnp.concatenate(
        [own_dk.reshape(shard_rows, kv_width), own_dv.reshape(shard_rows, kv_width)], axis=1
    ).astype(jnp.bfloat16)
    return_bundle = jnp.concatenate([dq_noisy, noisy_pair], axis=1)
    dq_noisy = return_bundle[:, :query_width]
    noisy_pair = return_bundle[:, query_width:]
    pair_grads = jnp.concatenate([clean_pair_grads, noisy_pair], axis=0)
    input_terms = jnp.einsum(
        "tc,rc->tr",
        pair_grads,
        lax.all_gather(weight_pair, CONTEXT, axis=0, tiled=True),
        preferred_element_type=jnp.float32,
    )
    grad_x = (
        summed_on_arrival(input_terms.astype(jnp.bfloat16), "head", 1)
        .astype(jnp.bfloat16)
        .reshape(tokens.shape)
    )
    columns = full_tokens
    weight_local = sum_by_axis(
        jnp.einsum("tr,tc->rc", columns, pair_grads, preferred_element_type=jnp.float32), CONTEXT
    )
    weight_sums = over_copies(weight_local.astype(jnp.bfloat16), "dp").astype(jnp.float32)
    grad_query = jnp.stack([dq_clean, dq_noisy])[None]
    return (grad_query, grad_x, weight_sums[:, :kv_width], weight_sums[:, kv_width:])


def solution(mesh):
    torus = Mesh(
        mesh.devices.reshape(mesh.shape["dp"], 4, 8, mesh.shape["head"]),
        ("dp", "context_0", "context_1", "head"),
    )
    in_specs = (
        P("dp", None, CONTEXT, "head"),
        P("dp", None, CONTEXT, "head"),
        P("dp", None, CONTEXT, "head"),
        P(CONTEXT, "head"),
        P(CONTEXT, "head"),
        P("dp"),
    )
    out_specs = (
        P("dp", None, CONTEXT, "head"),
        P("dp", None, CONTEXT, "head"),
        P(CONTEXT, "head"),
        P(CONTEXT, "head"),
    )
    return jax.shard_map(
        per_device, mesh=torus, in_specs=in_specs, out_specs=out_specs, check_vma=False
    )
```

profile of v0, /device:TPU:8, one launch (start us, length us, event | category | flops | bytes accessed | tf_op | source)
XLA Modules:
  0.0 507.5 jit_solution(627499071341025403)
XLA Ops:
  10.3 5.4 %all_to_all.20 = bf16[2,256,2048]{1,2,0:T(8,128)(2,1)S(1)} all-to-all(bf16[2,256,2048]{1,2,0:T(8,128)(2,1)S(1)} %broadcast_in_dim.134), channel_id=1, replica_groups=mesh['dp'=4,'context_0'=4,'context_1'=8,'head'=2] {'head'}, dimensions={0} | all-to-all | bytes 4194304 | tf_op jit(solution)/shard_map/all_to_all | solution.py:21
  15.7 75.1 %all-gather.3.cloned.1.call-done = bf16[4096,256]{1,0:T(8,128)(2,1)} async-done(((bf16[128,256]{1,0:T(8,128)(2,1)}), bf16[4096,256]{1,0:T(8,128)(2,1)}) %all-gather.3.cloned.1.call-update) | async-done | bytes 2097168 | tf_op jit(solution)/shard_map/all_gather | solution.py:136
  90.8 2.3 fusion.92
  94.9 7.3 %all-to-all-start.1 = ((bf16[32,128,256]{2,1,0:T(8,128)(2,1)}), bf16[32,128,256]{2,1,0:T(8,128)(2,1)}, u32[]{:S(2)}, u32[]{:S(2)}) async-start(bf16[32,128,256]{2,1,0:T(8,128)(2,1)} %broadcast_in_dim.135), calls=%async_computation.1 | async-start | bytes 4194304 | tf_op jit(solution)/shard_map/all_to_all | solution.py:21
  112.4 35.9 %all-to-all-done.1 = bf16[32,128,256]{2,1,0:T(8,128)(2,1)} async-done(((bf16[32,128,256]{2,1,0:T(8,128)(2,1)}), bf16[32,128,256]{2,1,0:T(8,128)(2,1)}, u32[]{:S(2)}, u32[]{:S(2)}) %all-to-all-start.1) | async-done | bytes 2097184 | tf_op jit(solution)/shard_map/all_to_all | solution.py:21
  148.3 3.1 slice_bitcast_fusion
  151.6 18.4 %conditional.5 = (f32[1,8,128]{2,1,0:T(8,128)}, f32[1,8,128]{2,1,0:T(8,128)S(1)}, f32[1,8,128,128]{3,2,1,0:T(8,128)S(1)}, f32[1,8,128]{2,1,0:T(8,128)}) conditional(s32[]{:T(128)} %convert_element_type.79, (f32[1,8,128]{2,1,0:T(8,128)}, f32[1,8,128]{2,1,0:T(8,128)S(1)}, f32[1,8,128,128]{3,2,1,0:T(8,128)S(1)}) %tuple.160, (s32[4096]{0:T(1024)S(1)}, ...), branch_computations={%region_6.7_spmd, %region_7.10_spmd} | conditional | flops 2202799104 | bytes 58019872 | solution.py:193
  153.6 3.7 fusion.25
  158.0 4.0 fusion.27
  163.3 6.0 %fusion.35 = f32[1,8,128,128]{3,2,1,0:T(8,128)S(1)} fusion(f32[4096,128,8]{1,0,2:T(8,128)S(1)} %get-tuple-element.709, f32[8,128]{1,0:T(8,128)S(1)} %bitcast.427, pred[128,4096]{0,1:T(8,128)(4,1)S(1)} %broadcast_compare_fusion.1, bf16[4096,1,128]{2,0,1:T(8,128)(2,1)} %get-tuple-element.377, f32[1,8,128,128]{3,2,1,0:T(8,128)S(1)} %get-tuple-element.376, ...), kind=kOutput, calls=%fused_computation.33 | convolution fusion | flops 1094975488 | bytes 19406848 | tf_op jit(solution)/shard_map/cond/branch_1_fun/kgij,jkd->kgid/dot_general | solution.py:80
  173.0 15.9 %conditional.4 = (f32[1,8,128]{2,1,0:T(8,128)S(1)}, f32[1,8,128]{2,1,0:T(8,128)S(1)}, f32[1,8,128,128]{3,2,1,0:T(8,128)S(1)}, f32[1,8,128]{2,1,0:T(8,128)S(1)}) conditional(s32[]{:T(128)} %convert_element_type.79, () %tuple.57, (s32[4096]{0:T(1024)S(1)}, s32[128,4096]{0,1:T(8,128)S(1)}, bf16[4096,1,128]{2,0,1:T(8,128)(2,1)}, ...), branch_computations={%region_0.1_spmd, %region_1.4_spmd} | conditional | flops 2202670080 | bytes 57479200 | solution.py:192
  174.8 3.8 fusion.4
  178.6 4.2 fusion.6
  182.9 6.0 %fusion.14 = f32[1,8,128,128]{3,2,1,0:T(8,128)S(1)} fusion(f32[4096,128,8]{1,0,2:T(8,128)S(1)} %get-tuple-element.707, f32[8,128]{1,0:T(8,128)S(1)} %get-tuple-element.705, pred[128,4096]{0,1:T(8,128)(4,1)S(1)} %broadcast_compare_fusion, bf16[4096,1,128]{2,0,1:T(8,128)(2,1)} %get-tuple-element.369, f32[8,128]{1,0:T(8,128)S(1)} %get-tuple-element.704), kind=kOutput, calls=%fused_computation.11 | convolution fusion | flops 1094844416 | bytes 18882560 | tf_op jit(solution)/shard_map/cond/branch_1_fun/kgij,jkd->kgid/dot_general | solution.py:80
  191.2 2.4 broadcast_in_dim.133.clone
  195.3 54.1 %while.20 = (s32[]{:T(128)}, f32[128,1,8,128]{3,0,2,1:T(8,128)}, f32[128,1,8,128]{3,0,2,1:T(8,128)}, f32[4096,256]{0,1:T(8,128)}, s32[]{:T(128)}, /*index=5*/s32...) while((s32[]{:T(128)}, f32[128,1,8,128]{3,0,2,1:T(8,128)}, ...), condition=%wide.region_15.16_spmd.clone.clone, body=%wide.region_10.15_spmd.clone.clone.sunk | while | flops 1350440704 | bytes 36462060 | solution.py:252
  198.1 4.5 conditional.13
  202.6 4.5 conditional.12
  216.2 4.5 conditional.13
  220.6 4.5 conditional.12
  234.2 4.5 conditional.13
  238.7 4.5 conditional.12
  249.4 4.0 convert_element_type.84
  253.4 119.5 %reduce-scatter.9.cloned.1.call-done = bf16[1024,256]{0,1:T(8,128)(2,1)} async-done(((bf16[4096,256]{0,1:T(8,128)(2,1)}), bf16[1024,256]{0,1:T(8,128)(2,1)}) %reduce-scatter.9.cloned.1.call-update) | async-done | bytes 524304 | tf_op jit(solution)/shard_map/reduce_scatter | solution.py:30
  372.9 2.1 copy.155
  376.1 37.6 %reduce-scatter.13.cloned.1.call-done = bf16[128,256]{1,0:T(8,128)(2,1)} async-done(((bf16[1024,256]{1,0:T(8,128)(2,1)}), bf16[128,256]{1,0:T(8,128)(2,1)}) %reduce-scatter.13.cloned.1.call-update) | async-done | bytes 65552
  414.7 2.1 fusion.81
  416.9 29.8 %reduce-scatter.11.cloned.1.call-done = bf16[1024,256]{0,1:T(8,128)(2,1)} async-done(((bf16[4096,256]{0,1:T(8,128)(2,1)}), bf16[1024,256]{0,1:T(8,128)(2,1)}) %reduce-scatter.11.cloned.1.call-update) | async-done | bytes 524304 | tf_op jit(solution)/shard_map/reduce_scatter | solution.py:49
  453.0 5.4 %all_to_all.21 = bf16[2,256,2048]{2,1,0:T(8,128)(2,1)S(1)} all-to-all(bf16[2,256,2048]{2,1,0:T(8,128)(2,1)S(1)} %bitcast.403), channel_id=1, replica_groups=mesh['dp'=4,'context_0'=4,'context_1'=8,'head'=2] {'head'}, dimensions={0} | all-to-all | bytes 4194304 | tf_op jit(solution)/shard_map/all_to_all | solution.py:42
  458.4 29.1 %reduce-scatter.15.cloned.1.call-done = bf16[128,256]{1,0:T(8,128)(2,1)} async-done(((bf16[1024,256]{1,0:T(8,128)(2,1)}), bf16[128,256]{1,0:T(8,128)(2,1)}) %reduce-scatter.15.cloned.1.call-update) | async-done | bytes 65552 | tf_op jit(solution)/shard_map/reduce_scatter | solution.py:49
  489.1 4.2 all-to-all-start.3
  496.2 3.8 all-to-all-done.3
  (192 shorter events, 94.9 us)
Async XLA Ops:
  7.2 83.7 %all-gather.3.cloned.1.call-start = ((), (), s32[]{:S(2)}) async-start(), calls=%async_computation.8 | async-start | bytes 2162688 | tf_op jit(solution)/shard_map/all_gather | solution.py:136
  15.7 79.2 %copy-start.4 = (bf16[2,256,2048]{1,2,0:T(8,128)(2,1)}, bf16[2,256,2048]{1,2,0:T(8,128)(2,1)S(1)}, u32[]{:S(2)}) copy-start(bf16[2,256,2048]{1,2,0:T(8,128)(2,1)S(1)} %all_to_all.20) | copy-start | bytes 6291460
  93.2 11.9 %copy-start.16 = (bf16[256,256]{0,1:T(8,128)(2,1)}, bf16[256,256]{0,1:T(8,128)(2,1)S(1)}, u32[]{:S(2)}) copy-start(bf16[256,256]{0,1:T(8,128)(2,1)S(1)} %fusion.92) | copy-start | bytes 393220
  93.2 10.5 %copy-start.15 = (bf16[1,2,128,1024]{3,2,1,0:T(8,128)(2,1)S(1)}, bf16[1,2,128,1024]{3,2,1,0:T(8,128)(2,1)}, u32[]{:S(2)}) copy-start(bf16[1,2,128,1024]{3,2,1,0:T(8,128)(2,1)} %param.17) | copy-start | bytes 1572868
  93.2 9.0 %copy-start.14 = (bf16[128,256]{0,1:T(8,128)(2,1)}, bf16[128,256]{0,1:T(8,128)(2,1)S(1)}, u32[]{:S(2)}) copy-start(bf16[128,256]{0,1:T(8,128)(2,1)S(1)} %slice.67) | copy-start | bytes 196612
  94.9 53.4 %all-to-all-start.1 = ((bf16[32,128,256]{2,1,0:T(8,128)(2,1)}), bf16[32,128,256]{2,1,0:T(8,128)(2,1)}, u32[]{:S(2)}, u32[]{:S(2)}) async-start(bf16[32,128,256]{2,1,0:T(8,128)(2,1)} %broadcast_in_dim.135), calls=%async_computation.1 | async-start | bytes 4194304 | tf_op jit(solution)/shard_map/all_to_all | solution.py:21
  102.2 89.0 %all-gather.5.cloned.1.call-start = ((), (), s32[]{:S(2)}) async-start(), calls=%async_computation.9 | async-start | bytes 2162688 | tf_op jit(solution)/shard_map/all_gather | solution.py:196
  103.0 269.9 %reduce-scatter.9.cloned.1.call-start = ((), (), s32[]{:S(2)}) async-start(), calls=%async_computation.10 | async-start | bytes 2621440 | tf_op jit(solution)/shard_map/reduce_scatter | solution.py:30
  103.9 47.7 %copy-start.8 = (bf16[1,1,128,1024]{2,3,1,0:T(8,128)(2,1)}, bf16[1,1,128,1024]{2,3,1,0:T(8,128)(2,1)S(1)}, u32[]{:S(2)}) copy-start(bf16[1,1,128,1024]{2,3,1,0:T(8,128)(2,1)S(1)} %copy.165) | copy-start | bytes 786436
  105.1 5.6 %copy-start.17 = (bf16[256,256]{0,1:T(8,128)(2,1)S(1)}, bf16[256,256]{0,1:T(8,128)(2,1)}, u32[]{:S(2)}) copy-start(bf16[256,256]{0,1:T(8,128)(2,1)} %copy-done.16) | copy-start | bytes 393220
  105.3 84.7 %copy-start.6 = (bf16[1,1,128,1024]{2,3,1,0:T(8,128)(2,1)}, bf16[1,1,128,1024]{2,3,1,0:T(8,128)(2,1)S(1)}, u32[]{:S(2)}) copy-start(bf16[1,1,128,1024]{2,3,1,0:T(8,128)(2,1)S(1)} %copy.166) | copy-start | bytes 786436
  105.5 2.1 copy-start.10
  109.9 0.8 copy-start.2
  148.3 3.1 copy-start.19
  148.3 3.2 copy-start.12
  148.3 3.2 copy-start.18
  249.4 126.0 %copy-start.3 = (f32[1,8,128,128]{2,3,1,0:T(8,128)S(1)}, f32[1,8,128,128]{2,3,1,0:T(8,128)}, u32[]{:S(2)}) copy-start(f32[1,8,128,128]{2,3,1,0:T(8,128)} %copy-done.2) | copy-start | bytes 1572868
  249.4 126.0 %copy-start.7 = (bf16[1,1,128,1024]{2,3,1,0:T(8,128)(2,1)S(1)}, bf16[1,1,128,1024]{2,3,1,0:T(8,128)(2,1)}, u32[]{:S(2)}) copy-start(bf16[1,1,128,1024]{2,3,1,0:T(8,128)(2,1)} %copy-done.6) | copy-start | bytes 786436
  249.4 126.2 %copy-start.9 = (bf16[1,1,128,1024]{2,3,1,0:T(8,128)(2,1)S(1)}, bf16[1,1,128,1024]{2,3,1,0:T(8,128)(2,1)}, u32[]{:S(2)}) copy-start(bf16[1,1,128,1024]{2,3,1,0:T(8,128)(2,1)} %copy-done.8) | copy-start | bytes 786436
  253.4 161.3 %copy-start.5 = (bf16[2,256,2048]{1,2,0:T(8,128)(2,1)S(1)}, bf16[2,256,2048]{1,2,0:T(8,128)(2,1)}, u32[]{:S(2)}) copy-start(bf16[2,256,2048]{1,2,0:T(8,128)(2,1)} %copy-done.4) | copy-start | bytes 6291460
  253.4 160.4 %reduce-scatter.13.cloned.1.call-start = ((), (), s32[]{:S(2)}) async-start(), calls=%async_computation.12 | async-start | bytes 589824
  375.0 71.7 %reduce-scatter.11.cloned.1.call-start = ((), (), s32[]{:S(2)}) async-start(), calls=%async_computation.11 | async-start | bytes 2621440 | tf_op jit(solution)/shard_map/reduce_scatter | solution.py:49
  376.1 72.7 %copy-start.1 = (f32[128,1,8,128]{3,0,2,1:T(8,128)S(1)}, f32[128,1,8,128]{3,0,2,1:T(8,128)}, u32[]{:S(2)}) copy-start(f32[128,1,8,128]{3,0,2,1:T(8,128)} %get-tuple-element.441) | copy-start | bytes 1572868
  414.7 35.1 %copy-start = (f32[128,1,8,128]{3,0,2,1:T(8,128)S(1)}, f32[128,1,8,128]{3,0,2,1:T(8,128)}, u32[]{:S(2)}) copy-start(f32[128,1,8,128]{3,0,2,1:T(8,128)} %get-tuple-element.440) | copy-start | bytes 1572868
  416.8 35.2 %copy-start.11 = (bf16[4096,256]{1,0:T(8,128)(2,1)S(1)}, bf16[4096,256]{1,0:T(8,128)(2,1)}, u32[]{:S(2)}) copy-start(bf16[4096,256]{1,0:T(8,128)(2,1)} %all-gather.3.cloned.1.call-done) | copy-start | bytes 6291460
  416.8 70.7 %reduce-scatter.15.cloned.1.call-start = ((), (), s32[]{:S(2)}) async-start(), calls=%async_computation.13 | async-start | bytes 589824 | tf_op jit(solution)/shard_map/reduce_scatter | solution.py:49
  452.7 40.6 %copy-start.13 = (bf16[128,1,8,128]{0,3,2,1:T(8,128)(2,1)S(1)}, bf16[128,1,8,128]{0,3,2,1:T(8,128)(2,1)}, u32[]{:S(2)}) copy-start(bf16[128,1,8,128]{0,3,2,1:T(8,128)(2,1)} %fusion.88) | copy-start | bytes 786436
  489.1 10.9 %all-to-all-start.3 = ((bf16[4,128,256]{2,1,0:T(8,128)(2,1)}), bf16[4,128,256]{2,1,0:T(8,128)(2,1)S(1)}, u32[]{:S(2)}, u32[]{:S(2)}) async-start(bf16[4,128,256]{2,1,0:T(8,128)(2,1)} %broadcast_in_dim.144), calls=%async_computation.5 | async-start | bytes 524288 | tf_op jit(solution)/shard_map/all_to_all | solution.py:21
Sparse Core Ops, SparseCore 0:
  11.2 79.6 all-gather.2
  106.1 83.5 all-gather.4
  253.5 119.3 reduce-scatter.8
  375.4 38.2 reduce-scatter.12
  417.0 29.7 reduce-scatter.10
  449.2 38.2 reduce-scatter.14
where the time goes:
time: 511 us; the launch traced here: 508 us
  waiting for transfers between devices  332 us (65%)
  matrix products  55.1 us (11%)
  other arithmetic  44.8 us (9%)
  local copies, waits for them, and re-layouts  37.4 us (7%)
  between operations  15.2 us (3%)
  starting transfers between devices  12 us (2%)
  blocking collectives  10.8 us (2%)
    reduce_scatter x1, waiting for transfers between devices, summed_rows(): array = lax.psum_scatter(array, axis, scatter_dimension=dim, tiled=True)  119 us
    all_gather x1, waiting for transfers between devices, per_device(): lax.all_gather(weight_pair, CONTEXT, axis=0, tiled=True)  75.1 us
    reduce_scatter x2, waiting for transfers between devices, sum_by_axis(): so_far = lax.psum_scatter(so_far, axis, scatter_dimension=0, tiled=True)  58.9 us
    all_to_all x2, waiting for transfers between devices, sent_to_all(): return lax.all_to_all(copies, axis, split_axis=0, concat_axis=0, tiled=True)  39.7 us
    unnamed x7, waiting for transfers between devices  38.4 us
    dot_general x9, matrix products, score_block(): jnp.einsum('ikgd,jkd->kgij', query_rows, key_rows, preferred_element_type...  17.7 us
    dot_general x3, matrix products, forward_step(): jnp.einsum('kgij,jkd->kgid', weights.astype(jnp.bfloat16), value_rows, pr...  13.1 us
    all_to_all x2, starting transfers between devices, sent_to_all(): return lax.all_to_all(copies, axis, split_axis=0, concat_axis=0, tiled=True)  11.5 us
  transfers between devices with their start and end apart: 8, of which 7 were waited for; matrix products, arithmetic and copies ran while one was open for 12% of the time, Pallas kernels for 0%

commit v1 on v0

--- a/solution.py
+++ b/solution.py
@@ -4,10 +4,19 @@
 from jax import lax
 from jax.sharding import Mesh
 from jax.sharding import PartitionSpec as P
+from jax.lax import all_to_all, axis_size
 
 HEAD_DIM = 128
 CONTEXT = ("context_0", "context_1")
 masked_score = -1e30
+
+
+def fix_orders_by_axis(page):
+    prior = axis_size(CONTEXT)
+    r1 = jnp.stack(prior * [page], axis=0)
+    block_now = all_to_all(r1, CONTEXT, 0, 0)
+    inter = jnp.concatenate(block_now, 0)
+    return inter
 
 
 def joined_along(tiles, dim):
@@ -132,9 +141,7 @@
     weight_pair = jnp.concatenate([w_key, w_value], axis=1)
     columns = full_tokens
     projected = jnp.dot(
-        columns,
-        lax.all_gather(weight_pair, CONTEXT, axis=0, tiled=True),
-        preferred_element_type=jnp.float32,
+        columns, fix_orders_by_axis(weight_pair), preferred_element_type=jnp.float32
     ).astype(jnp.bfloat16)
     clean_pairs = projected[:shard_rows]
     q_clean = queries[0, 0].reshape(shard_rows, kv_local, group_size, HEAD_DIM)

time: 511 us -> 577 us (1.13)
  blocking collectives: 10.8 us -> 65.8 us
  waiting for transfers between devices: 332 us -> 340 us
    all_to_all x1, blocking collectives: 5.42 us -> 60.4 us  [fix_orders_by_axis(): block_now = all_to_all(r1, CONTEXT, 0, 0)]
    all_to_all x2 -> x3, waiting for transfers between devices: 39.7 us -> 44.4 us  [sent_to_all(): return lax.all_to_all(copies, axis, split_axis=0, concat_axis=0, tiled=True)]
    all_to_all x2 -> x3, starting transfers between devices: 11.5 us -> 15.6 us  [sent_to_all(): return lax.all_to_all(copies, axis, split_axis=0, concat_axis=0, tiled=True)]
  transfers between devices with their start and end apart: 8 -> 9, of which waited for: 7 -> 8; matrix products, arithmetic and copies ran while one was open for 12% -> 11% of each run, Pallas kernels for 0% -> 0%
where the time goes in v1:
time: 577 us; the launch traced here: 574 us
  waiting for transfers between devices  340 us (59%)
  blocking collectives  65.8 us (11%)
  matrix products  54.7 us (9%)
  other arithmetic  43.3 us (8%)
  local copies, waits for them, and re-layouts  38.4 us (7%)
  starting transfers between devices  16.1 us (3%)
  between operations  15.3 us (3%)
    reduce_scatter x1, waiting for transfers between devices, summed_rows(): array = lax.psum_scatter(array, axis, scatter_dimension=dim, tiled=True)  120 us
    all_gather x1, waiting for transfers between devices, per_device(): lax.all_gather(weight_pair, CONTEXT, axis=0, tiled=True)  76.9 us
    all_to_all x1, blocking collectives, fix_orders_by_axis(): block_now = all_to_all(r1, CONTEXT, 0, 0)  60.4 us
    reduce_scatter x2, waiting for transfers between devices, sum_by_axis(): so_far = lax.psum_scatter(so_far, axis, scatter_dimension=0, tiled=True)  59.3 us
    all_to_all x3, waiting for transfers between devices, sent_to_all(): return lax.all_to_all(copies, axis, split_axis=0, concat_axis=0, tiled=True)  44.4 us
    unnamed x7, waiting for transfers between devices  39 us
    dot_general x9, matrix products, score_block(): jnp.einsum('ikgd,jkd->kgij', query_rows, key_rows, preferred_element_type...  17.7 us
    all_to_all x3, starting transfers between devices, sent_to_all(): return lax.all_to_all(copies, axis, split_axis=0, concat_axis=0, tiled=True)  15.6 us
  transfers between devices with their start and end apart: 9, of which 8 were waited for; matrix products, arithmetic and copies ran while one was open for 11% of the time, Pallas kernels for 0%

profile of v1, /device:TPU:8, one launch (start us, length us, event | category | flops | bytes accessed | tf_op | source)
XLA Modules:
  0.0 573.8 jit_solution(4197930967370982670)
XLA Ops:
  10.2 3.8 all-to-all-start.1
  14.0 2.8 all-to-all-done.1
  17.0 60.4 %all_to_all.25 = bf16[32,128,256]{2,1,0:T(8,128)(2,1)S(1)} all-to-all(bf16[32,128,256]{2,1,0:T(8,128)(2,1)S(1)} %stack.4), channel_id=1, replica_groups=mesh['dp'=4,'context_0'=4,'context_1'=8,'head'=2] {'context_0','context_1'}, dimensions={0} | all-to-all | bytes 4194304 | tf_op jit(solution)/shard_map/all_to_all | solution.py:17
  79.9 7.6 %all-to-all-start.2 = ((bf16[32,128,256]{2,1,0:T(8,128)(2,1)}), bf16[32,128,256]{2,1,0:T(8,128)(2,1)S(1)}, u32[]{:S(2)}, u32[]{:S(2)}) async-start(bf16[32,128,256]{2,1,0:T(8,128)(2,1)} %broadcast_in_dim.135), calls=%async_computation.2 | async-start | bytes 4194304 | tf_op jit(solution)/shard_map/all_to_all | solution.py:30
  99.5 37.9 %all-to-all-done.2 = bf16[32,128,256]{2,1,0:T(8,128)(2,1)S(1)} async-done(((bf16[32,128,256]{2,1,0:T(8,128)(2,1)}), bf16[32,128,256]{2,1,0:T(8,128)(2,1)S(1)}, u32[]{:S(2)}, u32[]{:S(2)}) %all-to-all-start.2) | async-done | bytes 2097184 | tf_op jit(solution)/shard_map/all_to_all | solution.py:30
  139.0 18.3 %conditional.5 = (f32[1,8,128]{2,1,0:T(8,128)}, f32[1,8,128]{2,1,0:T(8,128)S(1)}, f32[1,8,128,128]{3,2,1,0:T(8,128)S(1)}, f32[1,8,128]{2,1,0:T(8,128)}) conditional(s32[]{:T(128)} %convert_element_type.79, (f32[1,8,128]{2,1,0:T(8,128)}, f32[1,8,128]{2,1,0:T(8,128)S(1)}, f32[1,8,128,128]{3,2,1,0:T(8,128)S(1)}) %tuple.160, (s32[4096]{0:T(1024)S(1)}, ...), branch_computations={%region_6.7_spmd, %region_7.10_spmd} | conditional | flops 2202799104 | bytes 58019872 | solution.py:200
  141.1 3.7 fusion.25
  145.5 4.0 fusion.27
  150.8 6.0 %fusion.35 = f32[1,8,128,128]{3,2,1,0:T(8,128)S(1)} fusion(f32[4096,128,8]{1,0,2:T(8,128)S(1)} %get-tuple-element.709, f32[8,128]{1,0:T(8,128)S(1)} %bitcast.430, pred[128,4096]{0,1:T(8,128)(4,1)S(1)} %broadcast_compare_fusion.1, bf16[4096,1,128]{2,0,1:T(8,128)(2,1)} %get-tuple-element.377, f32[1,8,128,128]{3,2,1,0:T(8,128)S(1)} %get-tuple-element.376, ...), kind=kOutput, calls=%fused_computation.33 | convolution fusion | flops 1094975488 | bytes 19406848 | tf_op jit(solution)/shard_map/cond/branch_1_fun/kgij,jkd->kgid/dot_general | solution.py:89
  160.4 15.8 %conditional.4 = (f32[1,8,128]{2,1,0:T(8,128)S(1)}, f32[1,8,128]{2,1,0:T(8,128)S(1)}, f32[1,8,128,128]{3,2,1,0:T(8,128)S(1)}, f32[1,8,128]{2,1,0:T(8,128)S(1)}) conditional(s32[]{:T(128)} %convert_element_type.79, () %tuple.57, (s32[4096]{0:T(1024)S(1)}, s32[128,4096]{0,1:T(8,128)S(1)}, bf16[4096,1,128]{2,0,1:T(8,128)(2,1)}, ...), branch_computations={%region_0.1_spmd, %region_1.4_spmd} | conditional | flops 2202670080 | bytes 57479200 | solution.py:199
  162.2 3.7 fusion.4
  166.0 4.2 fusion.6
  170.3 5.9 %fusion.14 = f32[1,8,128,128]{3,2,1,0:T(8,128)S(1)} fusion(f32[4096,128,8]{1,0,2:T(8,128)S(1)} %get-tuple-element.707, f32[8,128]{1,0:T(8,128)S(1)} %get-tuple-element.705, pred[128,4096]{0,1:T(8,128)(4,1)S(1)} %broadcast_compare_fusion, bf16[4096,1,128]{2,0,1:T(8,128)(2,1)} %get-tuple-element.369, f32[8,128]{1,0:T(8,128)S(1)} %get-tuple-element.704), kind=kOutput, calls=%fused_computation.11 | convolution fusion | flops 1094844416 | bytes 18882560 | tf_op jit(solution)/shard_map/cond/branch_1_fun/kgij,jkd->kgid/dot_general | solution.py:89
  178.5 2.4 broadcast_in_dim.133.clone
  182.6 54.1 %while.20 = (s32[]{:T(128)}, f32[128,1,8,128]{3,0,2,1:T(8,128)}, f32[128,1,8,128]{3,0,2,1:T(8,128)}, f32[4096,256]{0,1:T(8,128)}, s32[]{:T(128)}, /*index=5*/s32...) while((s32[]{:T(128)}, f32[128,1,8,128]{3,0,2,1:T(8,128)}, ...), condition=%wide.region_15.16_spmd.clone.clone, body=%wide.region_10.15_spmd.clone.clone.sunk | while | flops 1350440704 | bytes 36462060 | solution.py:259
  185.5 4.5 conditional.13
  189.9 4.5 conditional.12
  203.5 4.5 conditional.13
  208.0 4.5 conditional.12
  221.6 4.5 conditional.13
  226.0 4.5 conditional.12
  236.8 4.0 convert_element_type.84
  240.8 119.8 %reduce-scatter.9.cloned.1.call-done = bf16[1024,256]{0,1:T(8,128)(2,1)} async-done(((bf16[4096,256]{0,1:T(8,128)(2,1)}), bf16[1024,256]{0,1:T(8,128)(2,1)}) %reduce-scatter.9.cloned.1.call-update) | async-done | bytes 524304 | tf_op jit(solution)/shard_map/reduce_scatter | solution.py:39
  360.6 2.1 copy.155
  363.8 37.8 %reduce-scatter.13.cloned.1.call-done = bf16[128,256]{1,0:T(8,128)(2,1)} async-done(((bf16[1024,256]{1,0:T(8,128)(2,1)}), bf16[128,256]{1,0:T(8,128)(2,1)}) %reduce-scatter.13.cloned.1.call-update) | async-done | bytes 65552
  405.3 29.2 %reduce-scatter.11.cloned.1.call-done = bf16[1024,256]{0,1:T(8,128)(2,1)} async-done(((bf16[4096,256]{0,1:T(8,128)(2,1)}), bf16[1024,256]{0,1:T(8,128)(2,1)}) %reduce-scatter.11.cloned.1.call-update) | async-done | bytes 524304 | tf_op jit(solution)/shard_map/reduce_scatter | solution.py:58
  438.7 76.9 %all-gather.5.cloned.1.call-done = bf16[4096,256]{1,0:T(8,128)(2,1)} async-done(((bf16[128,256]{1,0:T(8,128)(2,1)}), bf16[4096,256]{1,0:T(8,128)(2,1)}) %all-gather.5.cloned.1.call-update) | async-done | bytes 2097168 | tf_op jit(solution)/shard_map/all_gather | solution.py:286
  515.6 2.3 convolution_convert_fusion.1
  518.2 5.4 all_to_all.26
  523.6 30.1 %reduce-scatter.15.cloned.1.call-done = bf16[128,256]{1,0:T(8,128)(2,1)} async-done(((bf16[1024,256]{1,0:T(8,128)(2,1)}), bf16[128,256]{1,0:T(8,128)(2,1)}) %reduce-scatter.15.cloned.1.call-update) | async-done | bytes 65552 | tf_op jit(solution)/shard_map/reduce_scatter | solution.py:58
  555.3 4.2 all-to-all-start.4
  562.5 3.8 all-to-all-done.4
  (200 shorter events, 99.8 us)
Async XLA Ops:
  8.7 5.3 copy-start.19
  8.7 5.3 copy-start.20
  10.2 6.6 %all-to-all-start.1 = ((bf16[2,256,2048]{1,2,0:T(8,128)(2,1)}), bf16[2,256,2048]{1,2,0:T(8,128)(2,1)S(1)}, u32[]{:S(2)}, u32[]{:S(2)}) async-start(bf16[2,256,2048]{1,2,0:T(8,128)(2,1)} %broadcast_in_dim.134), calls=%async_computation.1 | async-start | bytes 4194304 | tf_op jit(solution)/shard_map/all_to_all | solution.py:30
  14.0 64.2 %copy-start.15 = (bf16[128,256]{1,0:T(8,128)(2,1)}, bf16[128,256]{1,0:T(8,128)(2,1)S(1)}, u32[]{:S(2)}) copy-start(bf16[128,256]{1,0:T(8,128)(2,1)S(1)} %constant_dynamic-update-slice_fusion.1) | copy-start | bytes 196612
  16.8 61.4 %copy-start.4 = (bf16[2,256,2048]{1,2,0:T(8,128)(2,1)}, bf16[2,256,2048]{1,2,0:T(8,128)(2,1)S(1)}, u32[]{:S(2)}) copy-start(bf16[2,256,2048]{1,2,0:T(8,128)(2,1)S(1)} %all-to-all-done.1) | copy-start | bytes 6291460
  78.2 12.9 %copy-start.16 = (bf16[256,256]{0,1:T(8,128)(2,1)}, bf16[256,256]{0,1:T(8,128)(2,1)S(1)}, u32[]{:S(2)}) copy-start(bf16[256,256]{0,1:T(8,128)(2,1)S(1)} %fusion.92) | copy-start | bytes 393220
  78.2 10.8 %copy-start.14 = (bf16[1,2,128,1024]{3,2,1,0:T(8,128)(2,1)S(1)}, bf16[1,2,128,1024]{3,2,1,0:T(8,128)(2,1)}, u32[]{:S(2)}) copy-start(bf16[1,2,128,1024]{3,2,1,0:T(8,128)(2,1)} %param.17) | copy-start | bytes 1572868
  78.2 9.4 %copy-start.13 = (bf16[128,256]{0,1:T(8,128)(2,1)}, bf16[128,256]{0,1:T(8,128)(2,1)S(1)}, u32[]{:S(2)}) copy-start(bf16[128,256]{0,1:T(8,128)(2,1)S(1)} %slice.67) | copy-start | bytes 196612
  79.9 57.5 %all-to-all-start.2 = ((bf16[32,128,256]{2,1,0:T(8,128)(2,1)}), bf16[32,128,256]{2,1,0:T(8,128)(2,1)S(1)}, u32[]{:S(2)}, u32[]{:S(2)}) async-start(bf16[32,128,256]{2,1,0:T(8,128)(2,1)} %broadcast_in_dim.135), calls=%async_computation.2 | async-start | bytes 4194304 | tf_op jit(solution)/shard_map/all_to_all | solution.py:30
  87.5 91.0 %all-gather.3.cloned.1.call-start = ((), (), s32[]{:S(2)}) async-start(), calls=%async_computation.9 | async-start | bytes 2162688 | tf_op jit(solution)/shard_map/all_gather | solution.py:203
  88.3 272.4 %reduce-scatter.9.cloned.1.call-start = ((), (), s32[]{:S(2)}) async-start(), calls=%async_computation.10 | async-start | bytes 2621440 | tf_op jit(solution)/shard_map/reduce_scatter | solution.py:39
  89.2 49.8 %copy-start.8 = (bf16[1,1,128,1024]{2,3,1,0:T(8,128)(2,1)}, bf16[1,1,128,1024]{2,3,1,0:T(8,128)(2,1)S(1)}, u32[]{:S(2)}) copy-start(bf16[1,1,128,1024]{2,3,1,0:T(8,128)(2,1)S(1)} %copy.165) | copy-start | bytes 786436
  91.1 6.7 %copy-start.17 = (bf16[256,256]{0,1:T(8,128)(2,1)S(1)}, bf16[256,256]{0,1:T(8,128)(2,1)}, u32[]{:S(2)}) copy-start(bf16[256,256]{0,1:T(8,128)(2,1)} %copy-done.16) | copy-start | bytes 393220
  91.3 86.1 %copy-start.6 = (bf16[1,1,128,1024]{2,3,1,0:T(8,128)(2,1)}, bf16[1,1,128,1024]{2,3,1,0:T(8,128)(2,1)S(1)}, u32[]{:S(2)}) copy-start(bf16[1,1,128,1024]{2,3,1,0:T(8,128)(2,1)S(1)} %copy.166) | copy-start | bytes 786436
  91.4 3.1 copy-start.10
  96.9 0.9 copy-start.2
  137.4 1.5 copy-start.21
  137.4 1.6 copy-start.11
  137.4 1.6 copy-start.18
  236.8 126.3 %copy-start.3 = (f32[1,8,128,128]{2,3,1,0:T(8,128)S(1)}, f32[1,8,128,128]{2,3,1,0:T(8,128)}, u32[]{:S(2)}) copy-start(f32[1,8,128,128]{2,3,1,0:T(8,128)} %copy-done.2) | copy-start | bytes 1572868
  236.8 126.3 %copy-start.7 = (bf16[1,1,128,1024]{2,3,1,0:T(8,128)(2,1)S(1)}, bf16[1,1,128,1024]{2,3,1,0:T(8,128)(2,1)}, u32[]{:S(2)}) copy-start(bf16[1,1,128,1024]{2,3,1,0:T(8,128)(2,1)} %copy-done.6) | copy-start | bytes 786436
  236.8 126.5 %copy-start.9 = (bf16[1,1,128,1024]{2,3,1,0:T(8,128)(2,1)S(1)}, bf16[1,1,128,1024]{2,3,1,0:T(8,128)(2,1)}, u32[]{:S(2)}) copy-start(bf16[1,1,128,1024]{2,3,1,0:T(8,128)(2,1)} %copy-done.8) | copy-start | bytes 786436
  240.8 161.8 %copy-start.5 = (bf16[2,256,2048]{1,2,0:T(8,128)(2,1)S(1)}, bf16[2,256,2048]{1,2,0:T(8,128)(2,1)}, u32[]{:S(2)}) copy-start(bf16[2,256,2048]{1,2,0:T(8,128)(2,1)} %copy-done.4) | copy-start | bytes 6291460
  240.8 160.8 %reduce-scatter.13.cloned.1.call-start = ((), (), s32[]{:S(2)}) async-start(), calls=%async_computation.13 | async-start | bytes 589824
  362.7 71.7 %reduce-scatter.11.cloned.1.call-start = ((), (), s32[]{:S(2)}) async-start(), calls=%async_computation.12 | async-start | bytes 2621440 | tf_op jit(solution)/shard_map/reduce_scatter | solution.py:58
  363.8 72.7 %copy-start.1 = (f32[128,1,8,128]{3,0,2,1:T(8,128)S(1)}, f32[128,1,8,128]{3,0,2,1:T(8,128)}, u32[]{:S(2)}) copy-start(f32[128,1,8,128]{3,0,2,1:T(8,128)} %get-tuple-element.441) | copy-start | bytes 1572868
  402.6 34.2 %copy-start = (f32[128,1,8,128]{3,0,2,1:T(8,128)S(1)}, f32[128,1,8,128]{3,0,2,1:T(8,128)}, u32[]{:S(2)}) copy-start(f32[128,1,8,128]{3,0,2,1:T(8,128)} %get-tuple-element.440) | copy-start | bytes 1572868
  404.7 110.9 %all-gather.5.cloned.1.call-start = ((), (), s32[]{:S(2)}) async-start(), calls=%async_computation.11 | async-start | bytes 2162688 | tf_op jit(solution)/shard_map/all_gather | solution.py:286
  405.3 148.5 %reduce-scatter.15.cloned.1.call-start = ((), (), s32[]{:S(2)}) async-start(), calls=%async_computation.14 | async-start | bytes 589824 | tf_op jit(solution)/shard_map/reduce_scatter | solution.py:58
  518.0 41.7 %copy-start.12 = (bf16[128,1,8,128]{0,3,2,1:T(8,128)(2,1)S(1)}, bf16[128,1,8,128]{0,3,2,1:T(8,128)(2,1)}, u32[]{:S(2)}) copy-start(bf16[128,1,8,128]{0,3,2,1:T(8,128)(2,1)} %fusion.88) | copy-start | bytes 786436
  555.3 10.9 %all-to-all-start.4 = ((bf16[4,128,256]{2,1,0:T(8,128)(2,1)}), bf16[4,128,256]{2,1,0:T(8,128)(2,1)S(1)}, u32[]{:S(2)}, u32[]{:S(2)}) async-start(bf16[4,128,256]{2,1,0:T(8,128)(2,1)} %broadcast_in_dim.144), calls=%async_computation.6 | async-start | bytes 524288 | tf_op jit(solution)/shard_map/all_to_all | solution.py:30
Sparse Core Ops, SparseCore 0:
  91.4 84.0 all-gather.2
  240.9 119.6 reduce-scatter.8
  363.3 38.2 reduce-scatter.12
  404.8 29.6 reduce-scatter.10
  437.8 77.7 all-gather.4
  518.1 35.6 reduce-scatter.14
